TPU v7x, 256 devices: a whole 4x4x8 slice. The times are simulated.
256 devices in a mesh: grp: 16 (over x, z_hi, core), mem: 16 (over z_lo, y).
Axes of the slice: x: 4, y: 4, z: 8 (z_hi: 2, z_lo: 4; z = z_hi * 4 + z_lo), core: 2. Of those that a mesh axis runs over, the one named last changes fastest.
Arguments:
- frames: bfloat16 [512, 256, 1024], P('grp', 'mem'), may hold values from -6 to 6
- probe_wave: float32 [2, 128, 128], P(None, 'mem'), may hold values from -6 to 6
Outputs:
- deconv_real: float32 [512, 256, 1024], P('mem', 'grp')
- deconv_imag: float32 [512, 256, 1024], P('mem', 'grp')
All inputs are finite; a program needn't handle non-finite values.
Results may differ from a plain program's by a relative error of at most 0.0087.
Values may be sent and summed in bfloat16 or wider, within the bound.
A program may use at most 128 MiB of HBM per device.

v0:
```python
import math

import jax
import jax.numpy as jnp
from jax import lax
from jax.sharding import PartitionSpec as P

WIN = 32
SCAN_Y = 512
SCAN_X = 256
STRIDE_Y = 4
STRIDE_X = 2


wiener_floor = 0.5


def scan_table(length):
    positions = jnp.arange(length, dtype=jnp.int32)
    phases = positions[:, None] * positions[None, :] % length
    angles = -2.0 * math.pi / length * phases.astype(jnp.float32)
    factor = 1.0 / math.sqrt(length)
    return (
        (jnp.cos(angles) * factor).astype(jnp.bfloat16),
        (jnp.sin(angles) * factor).astype(jnp.bfloat16),
    )


def detector_parts(window):
    offsets = jnp.arange(window, dtype=jnp.int32)
    phases = (
        offsets[:, None, None, None] * offsets[None, None, :, None]
        + offsets[None, :, None, None] * offsets[None, None, None, :]
    ) % window
    phases = phases.reshape(window * window, window * window)
    angles = -2.0 * math.pi / window * phases.astype(jnp.float32)
    factor = 1.0 / window
    return (
        (jnp.cos(angles) * factor).astype(jnp.bfloat16),
        (jnp.sin(angles) * factor).astype(jnp.bfloat16),
    )


def slab_table_of(part_re, part_im):
    upper = jnp.concatenate([part_re, part_im], axis=1)
    lower = jnp.concatenate([-part_im, part_re], axis=1)
    return jnp.concatenate([upper, lower], axis=0)


def block_columns(part_re, part_im, block_count):
    pixels = part_re.shape[0]
    block_width = pixels // block_count
    stacked = jnp.stack(
        [
            part_re.reshape(pixels, block_count, block_width),
            part_im.reshape(pixels, block_count, block_width),
        ],
        axis=2,
    )
    return stacked.reshape(pixels, 2 * pixels)


def signed_shift(freqs, length, step_size):
    centred = jnp.where(freqs >= length // 2, freqs - length, freqs)
    return jnp.floor_divide(centred, step_size)


def wigner_slab(probe_real, probe_imag, shift_y, shift_x, slab_table):
    grid_size = probe_real.shape[0]
    offsets = jnp.arange(WIN, dtype=jnp.int32)
    row_index = (offsets[None, :] + shift_y[:, None]) % grid_size
    col_index = (offsets[None, :] + shift_x[:, None]) % grid_size
    count_y = shift_y.shape[0]
    count_x = shift_x.shape[0]

    def shifted(plane):
        picked = jnp.take(plane, row_index, axis=0)
        picked = jnp.take(picked, col_index, axis=2)
        return picked.transpose(0, 2, 1, 3).reshape(count_y * count_x, WIN * WIN)

    moved_re = shifted(probe_real)
    moved_im = shifted(probe_imag)
    base_re = probe_real[:WIN, :WIN].reshape(1, WIN * WIN)
    base_im = probe_imag[:WIN, :WIN].reshape(1, WIN * WIN)
    prod_re = (base_re * moved_re + base_im * moved_im).astype(jnp.bfloat16)
    prod_im = (base_im * moved_re - base_re * moved_im).astype(jnp.bfloat16)
    stacked = jnp.concatenate([prod_re, prod_im], axis=1)
    slabs = jnp.dot(stacked, slab_table, preferred_element_type=jnp.float32)
    pixels = WIN * WIN
    slab_shape = (count_y, count_x, pixels)
    return (slabs[:, :pixels].reshape(slab_shape), slabs[:, pixels:].reshape(slab_shape))


def deconvolve(spec_re, spec_im, chi_re, chi_im):
    real_part = spec_re.astype(jnp.float32)
    imag_part = spec_im.astype(jnp.float32)
    denominator = chi_re * chi_re + chi_im * chi_im + wiener_floor
    out_re = (real_part * chi_re + imag_part * chi_im) / denominator
    out_im = (imag_part * chi_re - real_part * chi_im) / denominator
    return (out_re, out_im)


def swap_halves(values):
    half_width = values.shape[-1] // 2
    return jnp.concatenate([-values[..., half_width:], values[..., :half_width]], axis=-1)


def shards(frames, probe_wave):
    highest = lax.Precision.HIGHEST
    rows_dev, cols_dev, pixels = frames.shape
    det_re, det_im = detector_parts(WIN)
    cy_re, cy_im = scan_table(SCAN_Y)
    cx_re, cx_im = scan_table(SCAN_X)
    whole_probe = lax.all_gather(probe_wave, "mem", axis=1, tiled=True)
    flat_rows = frames.reshape(rows_dev * cols_dev, pixels)
    block_count = lax.axis_size("mem")
    merged = block_columns(det_re, det_im, block_count)
    spatial = jnp.dot(flat_rows, merged, preferred_element_type=jnp.float32).astype(jnp.bfloat16)
    spatial = spatial.reshape(rows_dev, cols_dev, 2 * pixels)
    received = lax.all_to_all(spatial, "mem", split_axis=2, concat_axis=1, tiled=True)
    first_term = jnp.einsum("nrc,rq->nqc", received, cx_re, preferred_element_type=jnp.float32)
    partial_x = first_term + jnp.einsum(
        "nrc,rq->nqc", swap_halves(received), cx_im, preferred_element_type=jnp.float32
    )
    gathered = lax.all_to_all(partial_x, "grp", split_axis=1, concat_axis=0, tiled=True)
    spectrum = jnp.einsum("rbc,rq->qbc", gathered, cy_re.astype(jnp.float32), precision=highest)
    spectrum = spectrum + jnp.einsum(
        "rbc,rq->qbc", swap_halves(gathered), cy_im.astype(jnp.float32), precision=highest
    )
    regrouped = lax.all_to_all(
        spectrum.astype(jnp.bfloat16), "mem", split_axis=0, concat_axis=2, tiled=True
    )
    qy_dev = regrouped.shape[0]
    qx_dev = regrouped.shape[1]
    unpacked = regrouped.reshape(qy_dev, qx_dev, block_count, 2, pixels // block_count)
    spec_re = unpacked[:, :, :, 0, :].reshape(qy_dev, qx_dev, pixels)
    spec_im = unpacked[:, :, :, 1, :].reshape(qy_dev, qx_dev, pixels)
    first_y = lax.axis_index("mem") * qy_dev
    first_x = lax.axis_index("grp") * qx_dev
    shift_y = signed_shift(
        first_y + STRIDE_Y * jnp.arange(qy_dev // STRIDE_Y, dtype=jnp.int32), SCAN_Y, STRIDE_Y
    )
    shift_x = signed_shift(
        first_x + STRIDE_X * jnp.arange(qx_dev // STRIDE_X, dtype=jnp.int32), SCAN_X, STRIDE_X
    )
    slab_table = slab_table_of(det_re, det_im)
    chi_re, chi_im = wigner_slab(whole_probe[0], whole_probe[1], shift_y, shift_x, slab_table)
    chi_re = jnp.repeat(jnp.repeat(chi_re, STRIDE_Y, axis=0), STRIDE_X, axis=1)
    chi_im = jnp.repeat(jnp.repeat(chi_im, STRIDE_Y, axis=0), STRIDE_X, axis=1)
    return deconvolve(spec_re, spec_im, chi_re, chi_im)


def solution(mesh):
    placed = (P("grp", "mem", None), P(None, "mem", None))
    return jax.shard_map(
        shards,
        mesh=mesh,
        in_specs=placed,
        out_specs=(P("mem", "grp", None), P("mem", "grp", None)),
        check_vma=False,
    )
```

profile of v0, /device:TPU:8, one launch (start us, length us, event | category | flops | bytes accessed | tf_op | source)
XLA Modules:
  0.0 437.5 jit_solution(3668463431823851423)
XLA Ops:
  0.7 8.0 %broadcast_add_fusion = s32[32,32,32,32]{1,0,3,2:T(8,128)} fusion(s32[32,32]{0,1:T(8,128)S(1)} %iota_multiply_fusion), kind=kLoop, calls=%fused_computation.12 | loop fusion | flops 1048576 | bytes 4198400 | tf_op jit(solution)/shard_map/add | solution.py:32
  8.7 13.7 %add.230 = s32[1024,16,1,64]{0,3,1,2:T(8,128)} reshape(s32[32,32,32,32]{1,0,3,2:T(8,128)} %broadcast_add_fusion) | data formatting | bytes 8388608 | tf_op jit(solution)/shard_map/add | solution.py:32
  22.3 18.0 %multiply_convert_fusion.3 = (bf16[1024,16,1,64]{0,3,1,2:T(8,128)(2,1)S(1)}, bf16[1024,16,1,64]{0,3,1,2:T(8,128)(2,1)S(1)}) fusion(s32[1024,16,1,64]{0,3,1,2:T(8,128)} %add.230), kind=kLoop, calls=%fused_computation.36 | loop fusion | flops 17825792 | bytes 8388608 | tf_op jit(solution)/shard_map/convert_element_type | solution.py:39
  43.8 9.3 %copy.30 = bf16[32,16,2048]{0,1,2:T(8,128)(2,1)} copy(bf16[32,16,2048]{2,1,0:T(8,128)(2,1)S(1)} %bitcast.95) | data formatting | bytes 4194304 | tf_op jit(solution)/shard_map/reshape | solution.py:119
  53.1 13.4 %reshape.296 = bf16[16,2,32768]{2,1,0:T(2,128)(2,1)S(1)} reshape(bf16[2048,16,32]{2,1,0:T(8,128)(2,1)} %bitcast.85) | data formatting | bytes 4194304
  66.5 56.5 %all_to_all.51 = bf16[16,2,32768]{2,1,0:T(2,128)(2,1)} all-to-all(bf16[16,2,32768]{2,1,0:T(2,128)(2,1)S(1)} %reshape.296), channel_id=1, replica_groups=mesh['grp'=16,'mem'=16] {'mem'}, dimensions={0} | all-to-all | bytes 4194304 | tf_op jit(solution)/shard_map/all_to_all | solution.py:120
  123.1 12.9 %reshape.297 = bf16[2048,16,32]{2,1,0:T(8,128)(2,1)} reshape(bf16[16,2,32768]{2,1,0:T(2,128)(2,1)} %all_to_all.51) | data formatting | bytes 4194304
  136.0 10.2 %copy.31 = bf16[32,16,16,128]{3,1,2,0:T(8,128)(2,1)S(1)} copy(bf16[32,16,16,128]{0,1,3,2:T(8,128)(2,1)} %bitcast.86) | data formatting | bytes 4194304 | tf_op jit(solution)/shard_map/all_to_all | solution.py:120
  151.2 4.4 %copy.32 = f32[32,256,128]{2,0,1:T(8,128)} copy(f32[32,256,128]{2,1,0:T(8,128)S(1)} %add_bitcast_fusion) | data formatting | bytes 8388608 | tf_op jit(solution)/shard_map/add | solution.py:122
  155.6 8.5 %all-to-all-start.1 = ((f32[32,256,128]{2,0,1:T(8,128)}), f32[32,256,128]{2,0,1:T(8,128)}, u32[]{:S(2)}, u32[]{:S(2)}) async-start(f32[32,256,128]{2,0,1:T(8,128)} %copy.32), calls=%async_computation.1 | async-start | bytes 8388608 | tf_op jit(solution)/shard_map/all_to_all | solution.py:125
  164.4 128.1 %all_gather.3 = f32[2,128,128]{2,1,0:T(8,128)S(1)} all-gather(f32[2,8,128]{2,1,0:T(8,128)S(1)} %copy-done.3), channel_id=1, replica_groups=mesh['grp'=16,'mem'=16] {'mem'}, dimensions={1}, use_global_device_ids=true | all-gather | bytes 139264 | tf_op jit(solution)/shard_map/all_gather | solution.py:114
  294.0 14.0 %add.248 = s32[1024,1024]{0,1:T(8,128)} reshape(s32[32,32,32,32]{1,0,3,2:T(8,128)} %broadcast_add_fusion) | data formatting | bytes 8388608 | tf_op jit(solution)/shard_map/add | solution.py:32
  310.8 7.7 %fusion.31 = f32[512,16,128]{2,0,1:T(8,128)S(1)} fusion(f32[512,16,128]{2,0,1:T(8,128)S(1)} %bitcast.83), kind=kOutput, calls=%fused_computation.61 | convolution fusion | flops 6446645248 | bytes 8388608 | tf_op jit(solution)/shard_map/rbc,rq->qbc/dot_general | solution.py:126
  320.0 8.7 %add_convert_fusion = bf16[512,16,128]{2,0,1:T(8,128)(2,1)S(1)} fusion(f32[512,16,128]{2,0,1:T(8,128)S(1)} %fusion.31, f32[512,16,64]{2,0,1:T(8,128)S(1)} %get-tuple-element.11, f32[512,16,64]{2,0,1:T(8,128)S(1)} %get-tuple-element.10), kind=kOutput, calls=%fused_computation.33 | convolution fusion | flops 6449790976 | bytes 10485760 | tf_op jit(solution)/shard_map/rbc,rq->qbc/dot_general | solution.py:127
  331.3 3.8 all-to-all-start.2
  354.9 16.5 %multiply_convert_fusion.1 = bf16[1024,1024]{0,1:T(8,128)(2,1)S(1)} fusion(s32[1024,1024]{0,1:T(8,128)} %add.248), kind=kLoop, calls=%fused_computation.32 | loop fusion | flops 15728640 | bytes 6291456 | tf_op jit(solution)/shard_map/convert_element_type | solution.py:39
  371.5 15.9 %fusion.88 = (bf16[1024,1024]{0,1:T(8,128)(2,1)S(1)}, bf16[1024,1024]{0,1:T(8,128)(2,1)S(1)}) fusion(s32[1024,1024]{0,1:T(8,128)S(1)} %copy-done.2), kind=kLoop, calls=%fused_computation.146 | loop fusion | flops 18874368 | bytes 8388608 | tf_op jit(solution)/shard_map/neg | solution.py:46
  392.3 3.7 reshape.230
  398.2 3.7 reshape.233
  401.9 3.5 reshape.225
  405.4 9.0 %fusion.89 = (bf16[32,16,16,1,64]{4,3,1,0,2:T(2,128)(2,1)S(1)}, bf16[32,16,16,1,64]{4,3,1,0,2:T(2,128)(2,1)S(1)}) fusion(bf16[32,16,16,2,64]{4,3,1,0,2:T(2,128)(2,1)} %reshape.225), kind=kLoop, calls=%fused_computation.147 | loop fusion | bytes 4194304 | tf_op jit(solution)/shard_map/slice | solution.py:136
  414.4 8.1 %copy_convert_fusion = (f32[32,16,16,1,64]{4,2,1,0,3:T(8,128)}, f32[32,16,16,1,64]{4,2,1,0,3:T(8,128)}) fusion(bf16[32,16,16,1,64]{4,3,1,0,2:T(2,128)(2,1)S(1)} %get-tuple-element.9, bf16[32,16,16,1,64]{4,3,1,0,2:T(2,128)(2,1)S(1)} %get-tuple-element.8), kind=kLoop, calls=%fused_computation.42 | loop fusion | flops 1048576 | bytes 6291456 | tf_op jit(solution)/shard_map/convert_element_type | solution.py:96
  426.0 4.9 %reshape.234 = f32[32,16,1024]{2,1,0:T(8,128)} reshape(f32[32,16,16,1,64]{4,2,1,0,3:T(8,128)} %get-tuple-element.27) | data formatting | bytes 4194304 | tf_op jit(solution)/shard_map/convert_element_type | solution.py:95
  430.9 6.1 %subtract_divide_fusion = (f32[32,16,1024]{2,1,0:T(8,128)}, f32[32,16,1024]{2,1,0:T(8,128)}) fusion(f32[32,16,1024]{2,1,0:T(8,128)} %reshape.234, f32[32,16,1024]{2,1,0:T(8,128)} %reshape.233, f32[32,16,1024]{2,1,0:T(8,128)S(1)} %reshape.235, f32[32,16,1024]{2,1,0:T(8,128)} %reshape.230), kind=kLoop, calls=%fused_computation.44 | loop fusion | flops 6291456 | bytes 12582912 | tf_op jit(solution)/shard_map/div | solution.py:99
  (55 shorter events, 47.3 us)
Async XLA Ops:
  0.6 40.8 %copy-start = (bf16[32,16,1024]{2,1,0:T(8,128)(2,1)S(1)}, bf16[32,16,1024]{2,1,0:T(8,128)(2,1)}, u32[]{:S(2)}) copy-start(bf16[32,16,1024]{2,1,0:T(8,128)(2,1)} %param.6) | copy-start | bytes 3145732
  155.6 8.7 %copy-start.3 = (f32[2,8,128]{2,1,0:T(8,128)S(1)}, f32[2,8,128]{2,1,0:T(8,128)}, u32[]{:S(2)}) copy-start(f32[2,8,128]{2,1,0:T(8,128)} %param.7) | copy-start | bytes 24580
  155.6 152.4 %all-to-all-start.1 = ((f32[32,256,128]{2,0,1:T(8,128)}), f32[32,256,128]{2,0,1:T(8,128)}, u32[]{:S(2)}, u32[]{:S(2)}) async-start(f32[32,256,128]{2,0,1:T(8,128)} %copy.32), calls=%async_computation.1 | async-start | bytes 8388608 | tf_op jit(solution)/shard_map/all_to_all | solution.py:125
  331.3 70.5 %all-to-all-start.2 = ((bf16[512,16,128]{2,1,0:T(8,128)(2,1)}), bf16[512,16,128]{2,1,0:T(8,128)(2,1)S(1)}, u32[]{:S(2)}, u32[]{:S(2)}) async-start(bf16[512,16,128]{2,1,0:T(8,128)(2,1)} %copy.34), calls=%async_computation.2 | async-start | bytes 4194304 | tf_op jit(solution)/shard_map/all_to_all | solution.py:130
  353.8 17.7 %copy-start.2 = (s32[1024,1024]{0,1:T(8,128)S(1)}, s32[1024,1024]{0,1:T(8,128)}, u32[]{:S(2)}) copy-start(s32[1024,1024]{0,1:T(8,128)} %add.248) | copy-start | bytes 12582916
  425.9 11.1 %copy-start.1 = (bf16[32,16,1024]{2,1,0:T(8,128)(2,1)S(1)}, bf16[32,16,1024]{2,1,0:T(8,128)(2,1)}, u32[]{:S(2)}) copy-start(bf16[32,16,1024]{2,1,0:T(8,128)(2,1)} %param.6) | copy-start | bytes 3145732
where the time goes:
time: 445 us; the launch traced here: 437 us
  blocking collectives  185 us (42%)
  local copies, waits for them, and re-layouts  132 us (30%)
  other arithmetic  81 us (18%)
  matrix products  25.6 us (6%)
  starting transfers between devices  12.3 us (3%)
    all_gather x1, blocking collectives, shards(): whole_probe = lax.all_gather(probe_wave, 'mem', axis=1, tiled=True)  128 us
    all_to_all x1, blocking collectives, shards(): lax.all_to_all(spatial, 'mem', split_axis=2, concat_axis=1, tiled=True)  56.5 us
    convert_element_type x2, other arithmetic, detector_parts(): (jnp.cos(angles) * factor).astype(jnp.bfloat16)  34.5 us
    add x2, local copies, waits for them, and re-layouts, detector_parts(): offsets[:, None, None, None] * offsets[None, None, :, None]  27.7 us
    unnamed x10, local copies, waits for them, and re-layouts  26.4 us
    neg x1, other arithmetic, slab_table_of(): lower = jnp.concatenate([-part_im, part_re], axis=1)  15.9 us
    all_to_all x1, local copies, waits for them, and re-layouts, shards(): lax.all_to_all(spatial, 'mem', split_axis=2, concat_axis=1, tiled=True)  10.2 us
    reshape x1, local copies, waits for them, and re-layouts, shards(): spatial = spatial.reshape(rows_dev, cols_dev, 2 * pixels)  9.29 us
  transfers between devices with their start and end apart: 2, of which 0 were waited for; matrix products, arithmetic and copies ran while one was open for 19% of the time, Pallas kernels for 0%

commit v1 on v0

v1 whole, which is shorter than its diff:
```python
import functools
import math

import jax
import jax.numpy as jnp
import ml_dtypes
import numpy as np
from jax import lax
from jax.experimental import pallas as pl
from jax.experimental.pallas import tpu as pltpu
from jax.sharding import PartitionSpec as P

WIN = 32
SCAN_Y = 512
SCAN_X = 256
PIX = 1024
MESH = pl.DeviceIdType.MESH
F32 = jnp.float32
BF16 = jnp.bfloat16

wiener_floor = 0.5


def scan_table(length):
    positions = np.arange(length)
    phases = (positions[:, None] * positions[None, :]) % length
    angles = -2.0 * math.pi / length * phases
    factor = 1.0 / math.sqrt(length)
    real = (np.cos(angles) * factor).astype(np.float32).astype(ml_dtypes.bfloat16)
    imag = (np.sin(angles) * factor).astype(np.float32).astype(ml_dtypes.bfloat16)
    return real, imag


def tables():
    yr, yi = scan_table(SCAN_Y)
    wy = np.concatenate([yr, yi], axis=1)
    xr, xi = scan_table(SCAN_X)
    wx = np.stack([np.concatenate([xr, -xi], axis=1), np.concatenate([xi, xr], axis=1)])
    perm = np.zeros((512, 512), ml_dtypes.bfloat16)
    src = np.arange(512)
    perm[src, (src // 32 % 4) * 128 + (src // 128) * 32 + src % 32] = 1
    pos = np.arange(WIN)
    angle = 2.0 * math.pi / WIN * (pos[:, None] * pos[None, :] % WIN)
    cos, sin = np.cos(angle), np.sin(angle)
    det = np.stack(
        [np.repeat(cos, WIN, 1), np.repeat(sin, WIN, 1), np.tile(cos, (1, WIN)) / WIN, np.tile(sin, (1, WIN)) / WIN]
    ).astype(np.float32)
    return wy, wx, perm, det


def dot(a, b):
    return jnp.dot(a, b, preferred_element_type=F32)


def arrange_frames(x, xs, ms, m1):
    for lt in range(8):
        xs[lt] = x[:, lt * 128 : (lt + 1) * 128].astype(F32)

    @pl.loop(0, 16)
    def _(xl):
        for dh in range(2):
            block = jnp.concatenate([xs[kk * 2 + dh, pl.ds(xl, 32, stride=16), :] for kk in range(4)], axis=0)
            ms[pl.ds(dh * 2048 + xl, 128, stride=16), :] = block.T

    m1[...] = ms[...].astype(BF16)


def detector_table(det, ddr, ddi):
    @pl.loop(0, 32)
    def _(ky):
        ca, sa = det[0, pl.ds(ky, 1), :], det[1, pl.ds(ky, 1), :]
        cb, sb = det[2], det[3]
        real = cb * ca - sb * sa
        imag = -(sb * ca + cb * sa)
        h = ky // 16
        upper = pl.multiple_of((ky % 16) * 32, 32)
        lower = pl.multiple_of(upper + 512, 32)
        ddr[h, pl.ds(upper, 32), :] = real.astype(BF16)
        ddr[h, pl.ds(lower, 32), :] = (-imag).astype(BF16)
        ddi[h, pl.ds(upper, 32), :] = imag.astype(BF16)
        ddi[h, pl.ds(lower, 32), :] = real.astype(BF16)


def probe_products(g, m, prb, pf):
    lane = lax.broadcasted_iota(jnp.int32, (8, 128), 1)
    row = lax.broadcasted_iota(jnp.int32, (8, 128), 0)
    group = lane // 32

    def flat(x, j):
        w = pltpu.roll(x, (128 - j) % 128, 1) if j else x
        y = w
        for q in range(1, 4):
            y = jnp.where(group == q, pltpu.roll(w, 32 * q, 1), y)
        return [jnp.sum(jnp.where(row == group + 4 * half, y, 0.0), axis=0, keepdims=True) for half in range(2)]

    base = []
    ext = []
    for c in range(2):
        tiles = []
        for q in range(4):
            tiles += flat(prb[q, c], 0)
        base.append([jnp.broadcast_to(t, (8, 128)) for t in tiles])
        tiles = []
        for q in range(5):
            x = pltpu.roll(prb[lax.rem(m + q, 16), c], lax.rem(128 - 8 * g, 128), 1)
            halves = [jnp.zeros((8, 128), F32)] * 2
            for j in range(8):
                sums = flat(x, j)
                halves = [jnp.where(row == j, jnp.broadcast_to(s, (8, 128)), h) for s, h in zip(sums, halves)]
            tiles += halves
        ext.append(tiles)
    for i in range(8):
        off, turn = i // 4, i % 4
        moved = []
        for c in range(2):
            if turn:
                rolled = [pltpu.roll(t, 128 - 32 * turn, 1) for t in ext[c]]
                moved.append([jnp.where(group < 4 - turn, rolled[t + off], rolled[t + off + 1]) for t in range(8)])
            else:
                moved.append([ext[c][t + off] for t in range(8)])
        for t in range(8):
            br, bi, mr, mi = base[0][t], base[1][t], moved[0][t], moved[1][t]
            h, at = t // 4, (t % 4) * 128
            pf[h, i * 8 : i * 8 + 8, at : at + 128] = br * mr + bi * mi
            pf[h, i * 8 : i * 8 + 8, 512 + at : 512 + at + 128] = bi * mr - br * mi


def wiener_gain(pf, ddr, ddi, gr, gi, ger, gei):
    left, right = pf[0].astype(BF16), pf[1].astype(BF16)
    chi_re = dot(left, ddr[0]) + dot(right, ddr[1])
    chi_im = dot(left, ddi[0]) + dot(right, ddi[1])
    scale = 1.0 / (chi_re * chi_re + chi_im * chi_im + wiener_floor)
    gr[...] = chi_re * scale
    gi[...] = chi_im * scale
    row = lax.broadcasted_iota(jnp.int32, (8, 1024), 0)

    @pl.loop(0, 8)
    def _(j):
        for src, dst in ((gr, ger), (gi, gei)):
            for t in range(4):
                first = jnp.broadcast_to(src[pl.ds(16 * t + j, 1), :], (8, 1024))
                second = jnp.broadcast_to(src[pl.ds(16 * t + 8 + j, 1), :], (8, 1024))
                dst[j, t * 8 : t * 8 + 8, :] = jnp.where(row < 4, first, second)


def scan_transform(h, r, rp, cst, f, m2, wy, wx, perm):
    if h == 0:

        @pl.loop(0, 4)
        def _(j):
            lhs = jnp.concatenate([r[pl.ds(pl.multiple_of((4 * j + t) * 256, 256), 256), :] for t in range(4)], axis=1)
            moved = dot(lhs, perm[...]).astype(BF16)
            for kk in range(4):
                rp[kk, j] = moved[:, kk * 128 : (kk + 1) * 128]

    @pl.loop(0, 2)
    def _(k2):
        kk = 2 * h + k2
        lhs = jnp.concatenate([rp[kk, j] for j in range(4)], axis=1)
        for c in range(2):
            cst[c * 256 : (c + 1) * 256, :] = dot(lhs, wy[:, c * 512 : (c + 1) * 512]).astype(BF16)
        for c in range(2):
            res = dot(wx[c], cst[...]).astype(BF16)
            for t in range(4):
                f[t, 2 * c + k2] = res[:, t * 128 : (t + 1) * 128]

    @pl.loop(0, 4)
    def _(t):
        lhs = jnp.concatenate([f[t, s] for s in range(4)], axis=1)
        res = dot(lhs, perm[...]).astype(BF16)
        for q in range(4):
            m2[h, 4 * t + q] = res[:, q * 128 : (q + 1) * 128]


def gather_pixels(h, r2, z, low):
    z[...] = r2[h].astype(F32)

    @pl.loop(0, 16)
    def _(v):
        halves = [z[pl.ds(dh * 2048 + v, 128, stride=16), :].T for dh in range(2)]
        turned = jnp.concatenate(halves, axis=1).astype(BF16)
        rows = jnp.concatenate([turned[s * 32 : (s + 1) * 32, :] for s in range(4)], axis=1)
        low[h, pl.ds(pl.multiple_of(v * 32, 32), 32), :] = rows


def kernel(
    frames, probe, wy_h, wx_h, perm_h, det_h, out_re, out_im,
    x, pv, prb, wy, wx, perm, det, xs, m1, r, rp, cst, f, m2, r2, low, ddr, ddi, pf, gr, gi, ger, gei, sre, sim, o,
    load_sem, prb_send, prb_recv, send, recv, out_sem,
):
    g, m = lax.axis_index("grp"), lax.axis_index("mem")
    me = g * 16 + m

    def peer(i):
        return lax.rem(g + i // 16, 16), lax.rem(m + lax.rem(i, 16), 16)

    loads = [
        pltpu.make_async_copy(src, dst, load_sem.at[n])
        for n, (src, dst) in enumerate(
            ((frames, x), (probe, pv), (wy_h, wy), (wx_h, wx), (perm_h, perm), (det_h, det))
        )
    ]
    for load in loads:
        load.start()
    barrier = pltpu.get_barrier_semaphore()

    @pl.loop(1, 256)
    def _(i):
        pl.semaphore_signal(barrier, inc=1, device_id=peer(i), device_id_type=MESH)

    loads[0].wait()
    loads[1].wait()
    arrange_frames(x, xs, o.at[0], m1)
    pl.semaphore_wait(barrier, 255)

    pltpu.make_async_copy(pv, prb.at[m], prb_recv).start()

    @pl.loop(1, 16)
    def _(i):
        pltpu.make_async_remote_copy(
            src_ref=pv, dst_ref=prb.at[m], send_sem=prb_send, recv_sem=prb_recv,
            device_id=(g, lax.rem(m + i, 16)), device_id_type=MESH,
        ).start()

    here = pl.ds(pl.multiple_of(me * 16, 16), 16)
    pltpu.make_async_copy(m1.at[here], r.at[here], recv.at[0]).start()

    @pl.loop(1, 256)
    def _(i):
        a, b = peer(i)
        there = pl.ds(pl.multiple_of((a * 16 + b) * 16, 16), 16)
        pltpu.make_async_remote_copy(
            src_ref=m1.at[there], dst_ref=r.at[here], send_sem=send.at[0], recv_sem=recv.at[0],
            device_id=(a, b), device_id_type=MESH,
        ).start()

    for load in loads[2:]:
        load.wait()
    detector_table(det, ddr, ddi)
    pltpu.make_async_copy(prb, prb, prb_recv).wait()
    probe_products(g, m, prb, pf)
    pltpu.make_async_copy(r, r, recv.at[0]).wait()

    for h in range(2):
        scan_transform(h, r, rp, cst, f, m2, wy, wx, perm)
        own = pl.ds(pl.multiple_of(g * 16, 16), 16)
        pltpu.make_async_copy(m2.at[h, m, own], r2.at[h, here], recv.at[1 + h]).start()

        @pl.loop(1, 256)
        def _(i):
            a, b = peer(i)
            there = pl.ds(pl.multiple_of(a * 16, 16), 16)
            pltpu.make_async_remote_copy(
                src_ref=m2.at[h, b, there], dst_ref=r2.at[h, here], send_sem=send.at[1 + h], recv_sem=recv.at[1 + h],
                device_id=(a, b), device_id_type=MESH,
            ).start()

    wiener_gain(pf, ddr, ddi, gr, gi, ger, gei)

    pltpu.make_async_copy(r2.at[0], r2.at[0], recv.at[1]).wait()
    gather_pixels(0, r2, o.at[0], low)

    @pl.loop(0, 4)
    def _(n):
        lanes = pl.ds(pl.multiple_of(n * 256, 256), 256)
        sre[n] = dot(low[0], ddr[0, :, lanes])
        sim[n] = dot(low[0], ddi[0, :, lanes])

    pltpu.make_async_copy(r2.at[1], r2.at[1], recv.at[2]).wait()
    gather_pixels(1, r2, o.at[0], low)
    oo = o

    @pl.loop(0, 4)
    def _(n):
        lanes = pl.ds(pl.multiple_of(n * 256, 256), 256)
        sre[n] += dot(low[1], ddr[1, :, lanes])
        sim[n] += dot(low[1], ddi[1, :, lanes])

        for lt in range(2):
            part = pl.ds(pl.multiple_of(n * 256 + lt * 128, 128), 128)

            @pl.loop(0, 16)
            def _(v):
                rows = pl.ds(pl.multiple_of(v * 32, 32), 32)
                s_re, s_im = sre[n, rows, lt * 128 : (lt + 1) * 128], sim[n, rows, lt * 128 : (lt + 1) * 128]
                g_re, g_im = ger[v // 2, :, part], gei[v // 2, :, part]
                spot = pl.ds((2 * n + lt) * 512 + v, 32, stride=16)
                oo[0, spot, :] = s_re * g_re + s_im * g_im
                oo[1, spot, :] = s_im * g_re - s_re * g_im

            block = pl.ds(pl.multiple_of((2 * n + lt) * 512, 512), 512)
            pltpu.make_async_copy(oo.at[0, block], out_re.at[:, part], out_sem.at[0]).start()
            pltpu.make_async_copy(oo.at[1, block], out_im.at[:, part], out_sem.at[1]).start()

    pltpu.make_async_copy(prb.at[pl.ds(0, 15)], prb.at[pl.ds(0, 15)], prb_send).wait()
    for n in range(3):
        sent = pl.ds(0, 255 * 16)
        pltpu.make_async_copy(r.at[sent], r.at[sent], send.at[n]).wait()
    pltpu.make_async_copy(oo.at[0], out_re, out_sem.at[0]).wait()
    pltpu.make_async_copy(oo.at[1], out_im, out_sem.at[1]).wait()


def fused(frames, probe):
    wy, wx, perm, det = (jnp.asarray(t) for t in tables())
    hbm = pl.BlockSpec(memory_space=pl.ANY)
    dma = pltpu.SemaphoreType.DMA
    return pl.pallas_call(
        kernel,
        out_shape=(jax.ShapeDtypeStruct((512, 1024), F32),) * 2,
        in_specs=[hbm] * 6,
        out_specs=(hbm, hbm),
        scratch_shapes=[
            pltpu.VMEM((512, 1024), BF16),
            pltpu.VMEM((2, 8, 128), F32),
            pltpu.VMEM((16, 2, 8, 128), F32),
            pltpu.VMEM((512, 1024), BF16),
            pltpu.VMEM((2, 256, 512), BF16),
            pltpu.VMEM((512, 512), BF16),
            pltpu.VMEM((4, 32, 1024), F32),
            pltpu.VMEM((8, 512, 128), F32),
            pltpu.VMEM((4096, 128), BF16),
            pltpu.VMEM((4096, 128), BF16),
            pltpu.VMEM((4, 4, 256, 128), BF16),
            pltpu.VMEM((512, 512), BF16),
            pltpu.VMEM((4, 4, 256, 128), BF16),
            pltpu.VMEM((2, 16, 256, 128), BF16),
            pltpu.VMEM((2, 4096, 128), BF16),
            pltpu.VMEM((2, 512, 1024), BF16),
            pltpu.VMEM((2, 1024, 1024), BF16),
            pltpu.VMEM((2, 1024, 1024), BF16),
            pltpu.VMEM((2, 64, 1024), F32),
            pltpu.VMEM((64, 1024), F32),
            pltpu.VMEM((64, 1024), F32),
            pltpu.VMEM((8, 32, 1024), F32),
            pltpu.VMEM((8, 32, 1024), F32),
            pltpu.VMEM((4, 512, 256), F32),
            pltpu.VMEM((4, 512, 256), F32),
            pltpu.VMEM((2, 4096, 128), F32),
            dma((6,)), dma, dma, dma((3,)), dma((3,)), dma((2,)),
        ],
        compiler_params=pltpu.CompilerParams(collective_id=0, has_side_effects=True, vmem_limit_bytes=60 << 20),
    )(frames, probe, wy, wx, perm, det)


def shards(frames, probe_wave):
    real, imag = fused(frames.reshape(512, PIX), probe_wave)
    return real.reshape(32, 16, PIX), imag.reshape(32, 16, PIX)


def solution(mesh):
    return jax.shard_map(
        shards,
        mesh=mesh,
        in_specs=(P("grp", "mem", None), P(None, "mem", None)),
        out_specs=(P("mem", "grp", None), P("mem", "grp", None)),
        check_vma=False,
    )
```

time: 445 us -> 116 us (0.26)
  the two profiles are of different devices: /device:TPU:8 before, /device:TPU:1 now
where the time goes in v1:
time: 116 us
  Pallas kernels  111 us (96%)
  local copies, waits for them, and re-layouts  4.63 us (4%)
    pallas_call x1, Pallas kernels, fused(): pl.pallas_call(kernel, out_shape=(jax.ShapeDtypeStruct((512, 1024), F32),...  111 us
    unnamed x4, local copies, waits for them, and re-layouts  4.63 us

profile of v1, /device:TPU:1, one launch (start us, length us, event | category | flops | bytes accessed | tf_op | source)
XLA Modules:
  0.0 115.8 jit_solution(1784167048608124539)
XLA Ops:
  0.6 110.5 %shard_map.77 = (f32[512,1024]{1,0:T(8,128)}, f32[512,1024]{1,0:T(8,128)}) custom-call(bf16[512,1024]{1,0:T(8,128)(2,1)} %bitcast.5, f32[2,8,128]{2,1,0:T(8,128)} %probe.1, bf16[512,1024]{1,0:T(8,128)(2,1)} %constant.8.clone.wy_h, bf16[2,256,512]{2,1,0:T(8,128)(2,1)} %constant.9.clone.wx_h, bf16[512,512]{1,0:T(8,128)(2,1)} %constant.10.clone.perm_h, ...), custom_call_target="tpu_custom_call" | custom-call | tf_op jit(solution)/shard_map/pallas_call | solution.py:307
  111.2 0.0 copy-start
  111.2 3.3 %copy.10 = f32[32,16,1024]{2,1,0:T(8,128)} copy(f32[32,16,1024]{2,1,0:T(8,128)} %bitcast.4) | data formatting | bytes 4194304
  114.5 0.0 copy-done
  114.5 1.3 %copy.11 = f32[32,16,1024]{2,1,0:T(8,128)} copy(f32[32,16,1024]{2,1,0:T(8,128)S(1)} %bitcast.3) | data formatting | bytes 4194304
Async XLA Ops:
  111.2 3.3 %copy-start = (f32[512,1024]{1,0:T(8,128)S(1)}, f32[512,1024]{1,0:T(8,128)}, u32[]{:S(2)}) copy-start(f32[512,1024]{1,0:T(8,128)} %get-tuple-element.5) | copy-start | bytes 6291460

commit v2 on v1

v2 whole, which is shorter than its diff:
```python
import math

import jax
import jax.numpy as jnp
import ml_dtypes
import numpy as np
from jax import lax
from jax.experimental import pallas as pl
from jax.experimental.pallas import tpu as pltpu
from jax.sharding import PartitionSpec as P

WIN = 32
SCAN_Y = 512
SCAN_X = 256
PIX = 1024
MESH = pl.DeviceIdType.MESH
F32 = jnp.float32
BF16 = jnp.bfloat16

wiener_floor = 0.5


def scan_table(length):
    positions = np.arange(length)
    phases = (positions[:, None] * positions[None, :]) % length
    angles = -2.0 * math.pi / length * phases
    factor = 1.0 / math.sqrt(length)
    real = (np.cos(angles) * factor).astype(np.float32).astype(ml_dtypes.bfloat16)
    imag = (np.sin(angles) * factor).astype(np.float32).astype(ml_dtypes.bfloat16)
    return real, imag


def tables():
    yr, yi = scan_table(SCAN_Y)
    wy = np.concatenate([yr, yi], axis=1)
    xr, xi = scan_table(SCAN_X)
    order = np.arange(SCAN_X).reshape(16, 8, 2).transpose(2, 0, 1).reshape(-1)
    xr, xi = xr[:, order], xi[:, order]
    wx = np.stack([np.concatenate([xr, -xi], axis=1), np.concatenate([xi, xr], axis=1)])
    perm = np.zeros((512, 512), ml_dtypes.bfloat16)
    src = np.arange(512)
    perm[src, (src // 32 % 4) * 128 + (src // 128) * 32 + src % 32] = 1
    pos = np.arange(WIN)
    angle = 2.0 * math.pi / WIN * (pos[:, None] * pos[None, :] % WIN)
    cos, sin = np.cos(angle), np.sin(angle)
    det = np.stack(
        [np.repeat(cos, WIN, 1), np.repeat(sin, WIN, 1), np.tile(cos, (1, WIN)) / WIN, np.tile(sin, (1, WIN)) / WIN]
    ).astype(np.float32)
    return wy, wx, perm, det


def dot(a, b):
    return jnp.dot(a, b, preferred_element_type=F32)


def arrange_frames(h, x, xs, ms, m1):
    for lt in range(4):
        xs[lt] = x[:, h * 512 + lt * 128 : h * 512 + (lt + 1) * 128].astype(F32)

    @pl.loop(0, 8)
    def _(x8):
        for dh in range(2):
            block = jnp.concatenate(
                [xs[k2 * 2 + dh, pl.ds(2 * x8 + x2, 32, stride=16), :] for k2 in range(2) for x2 in range(2)], axis=0
            )
            ms[pl.ds(dh * 1024 + x8, 128, stride=8), :] = block.T

    m1[h] = ms[0:2048, :].reshape(256, 8, 128).astype(BF16)


def detector_table(det, ddr, ddi):
    @pl.loop(0, 32)
    def _(ky):
        ca, sa = det[0, pl.ds(ky, 1), :], det[1, pl.ds(ky, 1), :]
        cb, sb = det[2], det[3]
        real = cb * ca - sb * sa
        imag = -(sb * ca + cb * sa)
        h = ky // 16
        upper = pl.multiple_of((ky % 16) * 32, 32)
        lower = pl.multiple_of(upper + 512, 32)
        ddr[h, pl.ds(upper, 32), :] = real.astype(BF16)
        ddr[h, pl.ds(lower, 32), :] = (-imag).astype(BF16)
        ddi[h, pl.ds(upper, 32), :] = imag.astype(BF16)
        ddi[h, pl.ds(lower, 32), :] = real.astype(BF16)


def probe_products(g, m, prb, pf):
    lane = lax.broadcasted_iota(jnp.int32, (8, 128), 1)
    row = lax.broadcasted_iota(jnp.int32, (8, 128), 0)
    group = lane // 32

    def flat(x, j):
        w = pltpu.roll(x, (128 - j) % 128, 1) if j else x
        y = w
        for q in range(1, 4):
            y = jnp.where(group == q, pltpu.roll(w, 32 * q, 1), y)
        return [jnp.sum(jnp.where(row == group + 4 * half, y, 0.0), axis=0, keepdims=True) for half in range(2)]

    base = []
    ext = []
    for c in range(2):
        tiles = []
        for q in range(4):
            tiles += flat(prb[q, c], 0)
        base.append([jnp.broadcast_to(t, (8, 128)) for t in tiles])
        tiles = []
        for q in range(5):
            x = pltpu.roll(prb[lax.rem(m + q, 16), c], lax.rem(128 - 8 * g, 128), 1)
            halves = [jnp.zeros((8, 128), F32)] * 2
            for j in range(8):
                sums = flat(x, j)
                halves = [jnp.where(row == j, jnp.broadcast_to(s, (8, 128)), h) for s, h in zip(sums, halves)]
            tiles += halves
        ext.append(tiles)
    for i in range(8):
        off, turn = i // 4, i % 4
        moved = []
        for c in range(2):
            if turn:
                rolled = [pltpu.roll(t, 128 - 32 * turn, 1) for t in ext[c]]
                moved.append([jnp.where(group < 4 - turn, rolled[t + off], rolled[t + off + 1]) for t in range(8)])
            else:
                moved.append([ext[c][t + off] for t in range(8)])
        for t in range(8):
            br, bi, mr, mi = base[0][t], base[1][t], moved[0][t], moved[1][t]
            h, at = t // 4, (t % 4) * 128
            pf[h, i * 8 : i * 8 + 8, at : at + 128] = br * mr + bi * mi
            pf[h, i * 8 : i * 8 + 8, 512 + at : 512 + at + 128] = bi * mr - br * mi


def wiener_gain(pf, ddr, ddi, gain):
    left, right = pf[0].astype(BF16), pf[1].astype(BF16)
    chi_re = dot(left, ddr[0]) + dot(right, ddr[1])
    chi_im = dot(left, ddi[0]) + dot(right, ddi[1])
    scale = 1.0 / (chi_re * chi_re + chi_im * chi_im + wiener_floor)
    gain[0] = chi_re * scale
    gain[1] = chi_im * scale


def scan_transform(h, r, rp, cst, f, store, wy, wx, perm):
    @pl.loop(0, 4)
    def _(j):
        parts = [r[h, pl.ds((4 * j + t) * 16, 16)].astype(F32).reshape(128, 128) for t in range(4)]
        moved = dot(jnp.concatenate(parts, axis=1).astype(BF16), perm[...]).astype(BF16)
        for s in range(4):
            rp[s, j] = moved[:, s * 128 : (s + 1) * 128]

    @pl.loop(0, 2)
    def _(k2):
        lhs = jnp.concatenate(
            [jnp.concatenate([rp[2 * k2 + x2, j] for j in range(4)], axis=1) for x2 in range(2)], axis=0
        )
        for c in range(2):
            cst[c * 256 : (c + 1) * 256, :] = dot(lhs, wy[:, c * 512 : (c + 1) * 512]).astype(BF16)
        for c in range(2):
            res = dot(wx[c], cst[...]).astype(BF16)
            for t in range(4):
                f[t, 2 * c + k2] = res[:, t * 128 : (t + 1) * 128]

    @pl.loop(0, 4)
    def _(t):
        lhs = jnp.concatenate([f[t, s] for s in range(4)], axis=1)
        res = dot(lhs, perm[...])
        for q in range(4):
            store(4 * t + q, res[:, q * 128 : (q + 1) * 128])


def gather_pixels(z, count, low, first):
    @pl.loop(0, count)
    def _(v):
        halves = [z[pl.ds(dh * 128 * count + v, 128, stride=count), :].T for dh in range(2)]
        turned = jnp.concatenate(halves, axis=1).astype(BF16)
        rows = jnp.concatenate([turned[s * 32 : (s + 1) * 32, :] for s in range(4)], axis=1)
        low[pl.ds(pl.multiple_of(first + v * 32, 32), 32), :] = rows


def exchange_kernel(
    frames, probe, wy_h, wx_h, perm_h, det_h, spec_out, gain_out,
    x, pv, prb, wy, wx, perm, det, xs, z, m1, r, rp, cst, f, m2, m3, r2, r3, low, ddr, ddi, pf, gain, sre, sim, spec,
    load_sem, prb_send, prb_recv, send, recv, out_sem,
):
    g, m = lax.axis_index("grp"), lax.axis_index("mem")
    me = g * 16 + m

    def to_all(act):
        @pl.loop(1, 16)
        def _(i):
            act(g, lax.rem(m + i, 16))

        @pl.loop(1, 16)
        def _(i):
            a = lax.rem(g + i, 16)

            @pl.loop(0, 16)
            def _(j):
                act(a, lax.rem(m + j, 16))

    def push(n, src, dst, a, b):
        pltpu.make_async_remote_copy(
            src_ref=src, dst_ref=dst, send_sem=send.at[n], recv_sem=recv.at[n], device_id=(a, b), device_id_type=MESH
        ).start()

    def arrived(n, ref):
        pltpu.make_async_copy(ref, ref, recv.at[n]).wait()

    loads = [
        pltpu.make_async_copy(src, dst, load_sem.at[n])
        for n, (src, dst) in enumerate(
            ((frames, x), (probe, pv), (wy_h, wy), (wx_h, wx), (perm_h, perm), (det_h, det))
        )
    ]
    for load in loads:
        load.start()
    barrier = pltpu.get_barrier_semaphore()
    to_all(lambda a, b: pl.semaphore_signal(barrier, inc=1, device_id=(a, b), device_id_type=MESH))

    loads[0].wait()
    loads[1].wait()
    for h in range(2):
        arrange_frames(h, x, xs, z, m1)
    pl.semaphore_wait(barrier, 255)

    for h in range(2):
        pltpu.make_async_copy(m1.at[h, me], r.at[h, me], recv.at[h]).start()
        to_all(lambda a, b: push(h, m1.at[h, a * 16 + b], r.at[h, me], a, b))
        if h == 0:
            pltpu.make_async_copy(pv, prb.at[m], prb_recv).start()

            @pl.loop(1, 16)
            def _(i):
                pltpu.make_async_remote_copy(
                    src_ref=pv, dst_ref=prb.at[m], send_sem=prb_send, recv_sem=prb_recv,
                    device_id=(g, lax.rem(m + i, 16)), device_id_type=MESH,
                ).start()

    for load in loads[2:]:
        load.wait()

    arrived(0, r.at[0])

    def store_first(b, tile):
        m2[b] = tile.astype(BF16)

    scan_transform(0, r, rp, cst, f, store_first, wy, wx, perm)
    here = pl.ds(pl.multiple_of(me * 16, 16), 16)
    pltpu.make_async_copy(m2.at[m, pl.ds(pl.multiple_of(g * 16, 16), 16)], r2.at[here], recv.at[2]).start()
    to_all(lambda a, b: push(2, m2.at[b, pl.ds(pl.multiple_of(a * 16, 16), 16)], r2.at[here], a, b))

    arrived(1, r.at[1])

    def store_second(b, tile):
        m3[b] = tile.reshape(32, 8, 128).astype(BF16)

    scan_transform(1, r, rp, cst, f, store_second, wy, wx, perm)
    for half in range(2):
        pltpu.make_async_copy(m3.at[m, 2 * g + half], r3.at[half, me], recv.at[3 + half]).start()
        to_all(lambda a, b: push(3 + half, m3.at[b, 2 * a + half], r3.at[half, me], a, b))

    detector_table(det, ddr, ddi)
    pltpu.make_async_copy(prb, prb, prb_recv).wait()
    probe_products(g, m, prb, pf)
    wiener_gain(pf, ddr, ddi, gain)
    gain_copy = pltpu.make_async_copy(gain, gain_out, out_sem.at[0])
    gain_copy.start()

    arrived(2, r2)
    z[...] = r2[...].astype(F32)
    gather_pixels(z, 16, low, 0)

    @pl.loop(0, 4)
    def _(n):
        lanes = pl.ds(pl.multiple_of(n * 256, 256), 256)
        sre[n] = dot(low[...], ddr[0, :, lanes])
        sim[n] = dot(low[...], ddi[0, :, lanes])

    copies = []
    for half in range(2):
        arrived(3 + half, r3.at[half])
        z[0:2048, :] = r3[half].astype(F32).reshape(2048, 128)
        gather_pixels(z, 8, low, half * 256)
        rows = slice(half * 256, (half + 1) * 256)

        @pl.loop(0, 4)
        def _(n):
            lanes = pl.ds(pl.multiple_of(n * 256, 256), 256)
            spec[0, rows, lanes] = (sre[n, rows, :] + dot(low[rows, :], ddr[1, :, lanes])).astype(BF16)
            spec[1, rows, lanes] = (sim[n, rows, :] + dot(low[rows, :], ddi[1, :, lanes])).astype(BF16)

        copies.append(pltpu.make_async_copy(spec.at[:, rows], spec_out.at[:, rows], out_sem.at[1 + half]))
        copies[-1].start()

    pltpu.make_async_copy(prb.at[pl.ds(0, 15)], prb.at[pl.ds(0, 15)], prb_send).wait()
    for n, ref in enumerate((r.at[0], r.at[1], None, r3.at[0], r3.at[1])):
        ref = r2.at[pl.ds(0, 255 * 16)] if ref is None else ref.at[pl.ds(0, 255)]
        pltpu.make_async_copy(ref, ref, send.at[n]).wait()
    gain_copy.wait()
    for copy in copies:
        copy.wait()


def exchange(frames, probe):
    wy, wx, perm, det = (jnp.asarray(t) for t in tables())
    hbm = pl.BlockSpec(memory_space=pl.ANY)
    dma = pltpu.SemaphoreType.DMA
    return pl.pallas_call(
        exchange_kernel,
        out_shape=(jax.ShapeDtypeStruct((2, 512, 1024), BF16), jax.ShapeDtypeStruct((2, 64, 1024), F32)),
        in_specs=[hbm] * 6,
        out_specs=(hbm, hbm),
        scratch_shapes=[
            pltpu.VMEM((512, 1024), BF16),
            pltpu.VMEM((2, 8, 128), F32),
            pltpu.VMEM((16, 2, 8, 128), F32),
            pltpu.VMEM((512, 1024), BF16),
            pltpu.VMEM((2, 256, 512), BF16),
            pltpu.VMEM((512, 512), BF16),
            pltpu.VMEM((4, 32, 1024), F32),
            pltpu.VMEM((4, 512, 128), F32),
            pltpu.VMEM((4096, 128), F32),
            pltpu.VMEM((2, 256, 8, 128), BF16),
            pltpu.VMEM((2, 256, 8, 128), BF16),
            pltpu.VMEM((4, 4, 128, 128), BF16),
            pltpu.VMEM((512, 512), BF16),
            pltpu.VMEM((4, 4, 256, 128), BF16),
            pltpu.VMEM((16, 256, 128), BF16),
            pltpu.VMEM((16, 32, 8, 128), BF16),
            pltpu.VMEM((4096, 128), BF16),
            pltpu.VMEM((2, 256, 8, 128), BF16),
            pltpu.VMEM((512, 1024), BF16),
            pltpu.VMEM((2, 1024, 1024), BF16),
            pltpu.VMEM((2, 1024, 1024), BF16),
            pltpu.VMEM((2, 64, 1024), F32),
            pltpu.VMEM((2, 64, 1024), F32),
            pltpu.VMEM((4, 512, 256), F32),
            pltpu.VMEM((4, 512, 256), F32),
            pltpu.VMEM((2, 512, 1024), BF16),
            dma((6,)), dma, dma, dma((5,)), dma((5,)), dma((3,)),
        ],
        compiler_params=pltpu.CompilerParams(collective_id=0, has_side_effects=True, vmem_limit_bytes=60 << 20),
    )(frames, probe, wy, wx, perm, det)


def quotient_kernel(spec, gain, out_re, out_im):
    row = lax.broadcasted_iota(jnp.int32, (8, 128), 0)

    @pl.loop(0, 8)
    def _(j):
        gains = []
        for c in range(2):
            tiles = []
            for t in range(4):
                first = jnp.broadcast_to(gain[c, pl.ds(16 * t + j, 1), :], (8, 128))
                second = jnp.broadcast_to(gain[c, pl.ds(16 * t + 8 + j, 1), :], (8, 128))
                tiles.append(jnp.where(row < 4, first, second))
            gains.append(jnp.concatenate(tiles, axis=0))
        g_re, g_im = gains
        for w in range(2):
            v = 2 * j + w
            rows = pl.ds(pl.multiple_of(v * 32, 32), 32)
            s_re, s_im = spec[0, rows, :].astype(F32), spec[1, rows, :].astype(F32)
            out_re[pl.ds(v, 32, stride=16), :] = s_re * g_re + s_im * g_im
            out_im[pl.ds(v, 32, stride=16), :] = s_im * g_re - s_re * g_im


def quotient(spec, gain):
    return pl.pallas_call(
        quotient_kernel,
        grid=(8,),
        out_shape=(jax.ShapeDtypeStruct((512, 1024), F32),) * 2,
        in_specs=[
            pl.BlockSpec((2, 512, 128), lambda n: (0, 0, n)),
            pl.BlockSpec((2, 64, 128), lambda n: (0, 0, n)),
        ],
        out_specs=(pl.BlockSpec((512, 128), lambda n: (0, n)),) * 2,
        compiler_params=pltpu.CompilerParams(vmem_limit_bytes=60 << 20),
    )(spec, gain)


def shards(frames, probe_wave):
    spec, gain = exchange(frames.reshape(512, PIX), probe_wave)
    real, imag = quotient(spec, gain)
    return real.reshape(32, 16, PIX), imag.reshape(32, 16, PIX)


def solution(mesh):
    return jax.shard_map(
        shards,
        mesh=mesh,
        in_specs=(P("grp", "mem", None), P(None, "mem", None)),
        out_specs=(P("mem", "grp", None), P("mem", "grp", None)),
        check_vma=False,
    )
```

time: 116 us -> 100 us (0.86)
  Pallas kernels: 111 us -> 99.5 us
  local copies, waits for them, and re-layouts: 4.63 us -> 0 us
    pallas_call x1 -> x2, Pallas kernels: 111 us -> 99.5 us  [the longest x1 92.5 us: exchange(): pl.pallas_call(exchange_kernel, out_shape=(jax.ShapeDtypeStruct((2, 512,...]
    unnamed x4 -> x0, local copies, waits for them, and re-layouts: 4.63 us -> none
where the time goes in v2:
time: 100 us
  Pallas kernels  99.5 us (100%)
    pallas_call x1, Pallas kernels, exchange(): pl.pallas_call(exchange_kernel, out_shape=(jax.ShapeDtypeStruct((2, 512,...  92.5 us
    pallas_call x1, Pallas kernels, quotient(): pl.pallas_call(quotient_kernel, grid=(8,), out_shape=(jax.ShapeDtypeStruc...  7.02 us

profile of v2, /device:TPU:1, one launch (start us, length us, event | category | flops | bytes accessed | tf_op | source)
XLA Modules:
  0.0 100.1 jit_solution(5014789113135920171)
XLA Ops:
  0.6 92.5 %shard_map.77 = (bf16[2,512,1024]{2,1,0:T(8,128)(2,1)}, f32[2,64,1024]{2,1,0:T(8,128)}) custom-call(bf16[512,1024]{1,0:T(8,128)(2,1)} %bitcast.3, f32[2,8,128]{2,1,0:T(8,128)} %probe.1, bf16[512,1024]{1,0:T(8,128)(2,1)} %constant.8.clone.wy_h, bf16[2,256,512]{2,1,0:T(8,128)(2,1)} %constant.9.clone.wx_h, bf16[512,512]{1,0:T(8,128)(2,1)} %constant.10.clone.perm_h, ...), custom_call_target="tpu_custom_call" | custom-call | tf_op jit(solution)/shard_map/pallas_call | solution.py:305
  93.1 7.0 %shard_map.78 = (f32[512,1024]{1,0:T(8,128)}, f32[512,1024]{1,0:T(8,128)}) custom-call(bf16[2,512,1024]{2,1,0:T(8,128)(2,1)} %get-tuple-element.6.spec, f32[2,64,1024]{2,1,0:T(8,128)} %get-tuple-element.7.gain), custom_call_target="tpu_custom_call" | custom-call | tf_op jit(solution)/shard_map/pallas_call | solution.py:366

commit v3 on v2

--- a/solution.py
+++ b/solution.py
@@ -40,13 +40,16 @@
     perm = np.zeros((512, 512), ml_dtypes.bfloat16)
     src = np.arange(512)
     perm[src, (src // 32 % 4) * 128 + (src // 128) * 32 + src % 32] = 1
+    rows = np.zeros((256, 256), ml_dtypes.bfloat16)
+    dst = np.arange(256)
+    rows[dst, (dst % 8) * 32 + dst // 8] = 1
     pos = np.arange(WIN)
     angle = 2.0 * math.pi / WIN * (pos[:, None] * pos[None, :] % WIN)
     cos, sin = np.cos(angle), np.sin(angle)
     det = np.stack(
         [np.repeat(cos, WIN, 1), np.repeat(sin, WIN, 1), np.tile(cos, (1, WIN)) / WIN, np.tile(sin, (1, WIN)) / WIN]
     ).astype(np.float32)
-    return wy, wx, perm, det
+    return wy, wx, perm, rows, det
 
 
 def dot(a, b):
@@ -128,13 +131,23 @@
             pf[h, i * 8 : i * 8 + 8, 512 + at : 512 + at + 128] = bi * mr - br * mi
 
 
-def wiener_gain(pf, ddr, ddi, gain):
+def wiener_gain(pf, ddr, ddi, chi, gain):
     left, right = pf[0].astype(BF16), pf[1].astype(BF16)
     chi_re = dot(left, ddr[0]) + dot(right, ddr[1])
     chi_im = dot(left, ddi[0]) + dot(right, ddi[1])
     scale = 1.0 / (chi_re * chi_re + chi_im * chi_im + wiener_floor)
-    gain[0] = chi_re * scale
-    gain[1] = chi_im * scale
+    chi[0] = chi_re * scale
+    chi[1] = chi_im * scale
+    row = lax.broadcasted_iota(jnp.int32, (8, 1024), 0) // 2
+
+    @pl.loop(0, 8)
+    def _(i):
+        for c in range(2):
+            for half in range(2):
+                tile = jnp.broadcast_to(chi[c, pl.ds(8 * i + 4 * half, 1), :], (8, 1024))
+                for j in range(1, 4):
+                    tile = jnp.where(row == j, chi[c, pl.ds(8 * i + 4 * half + j, 1), :], tile)
+                gain[c, i, half] = tile
 
 
 def scan_transform(h, r, rp, cst, f, store, wy, wx, perm):
@@ -165,35 +178,44 @@
             store(4 * t + q, res[:, q * 128 : (q + 1) * 128])
 
 
-def gather_pixels(z, count, low, first):
-    @pl.loop(0, count)
+def gather_pixels(z, count, half, raw, low, swap):
+    @pl.loop(0, 8)
     def _(v):
-        halves = [z[pl.ds(dh * 128 * count + v, 128, stride=count), :].T for dh in range(2)]
+        first = v + 8 * half if count == 16 else v
+        halves = [z[pl.ds(dh * 128 * count + first, 128, stride=count), :].T for dh in range(2)]
         turned = jnp.concatenate(halves, axis=1).astype(BF16)
         rows = jnp.concatenate([turned[s * 32 : (s + 1) * 32, :] for s in range(4)], axis=1)
-        low[pl.ds(pl.multiple_of(first + v * 32, 32), 32), :] = rows
+        raw[pl.ds(pl.multiple_of(v * 32, 32), 32), :] = rows
+
+    low[half * 256 : (half + 1) * 256, :] = dot(swap[...], raw[...]).astype(BF16)
 
 
 def exchange_kernel(
-    frames, probe, wy_h, wx_h, perm_h, det_h, spec_out, gain_out,
-    x, pv, prb, wy, wx, perm, det, xs, z, m1, r, rp, cst, f, m2, m3, r2, r3, low, ddr, ddi, pf, gain, sre, sim, spec,
+    frames, probe, wy_h, wx_h, perm_h, swap_h, det_h, spec_out, gain_out,
+    x, pv, prb, wy, wx, perm, swap, det, xs, z, m1, r, rp, cst, f, m2, m3, r2, r3, raw, low, ddr, ddi, pf, chi, gain, sre, sim, spec,
     load_sem, prb_send, prb_recv, send, recv, out_sem,
 ):
     g, m = lax.axis_index("grp"), lax.axis_index("mem")
     me = g * 16 + m
 
+    px, core, py = g // 4, lax.rem(g, 2), lax.rem(m, 4)
+    pz = lax.rem(g // 2, 2) * 4 + m // 4
+    turns = []
+    for dz in (4, 3, 5, 2, 6, 1, 7, 0):
+        z1 = lax.rem(pz + dz, 8)
+        turns.append(((z1 // 4) * 2, lax.rem(z1, 4) * 4))
+
     def to_all(act):
-        @pl.loop(1, 16)
+        @pl.loop(1, 32)
         def _(i):
-            act(g, lax.rem(m + i, 16))
-
-        @pl.loop(1, 16)
-        def _(i):
-            a = lax.rem(g + i, 16)
-
-            @pl.loop(0, 16)
-            def _(j):
-                act(a, lax.rem(m + j, 16))
+            step = 32 - i
+            a = lax.rem(px + lax.rem(step // 2, 4), 4) * 4 + lax.rem(core + lax.rem(step, 2), 2)
+            b = lax.rem(py + step // 8, 4)
+            for za, zb in turns:
+                act(a + za, b + zb)
+
+        for za, zb in turns[:-1]:
+            act(px * 4 + core + za, py + zb)
 
     def push(n, src, dst, a, b):
         pltpu.make_async_remote_copy(
@@ -206,7 +228,7 @@
     loads = [
         pltpu.make_async_copy(src, dst, load_sem.at[n])
         for n, (src, dst) in enumerate(
-            ((frames, x), (probe, pv), (wy_h, wy), (wx_h, wx), (perm_h, perm), (det_h, det))
+            ((frames, x), (probe, pv), (wy_h, wy), (wx_h, wx), (perm_h, perm), (swap_h, swap), (det_h, det))
         )
     ]
     for load in loads:
@@ -259,13 +281,14 @@
     detector_table(det, ddr, ddi)
     pltpu.make_async_copy(prb, prb, prb_recv).wait()
     probe_products(g, m, prb, pf)
-    wiener_gain(pf, ddr, ddi, gain)
+    wiener_gain(pf, ddr, ddi, chi, gain)
     gain_copy = pltpu.make_async_copy(gain, gain_out, out_sem.at[0])
     gain_copy.start()
 
     arrived(2, r2)
     z[...] = r2[...].astype(F32)
-    gather_pixels(z, 16, low, 0)
+    for half in range(2):
+        gather_pixels(z, 16, half, raw, low, swap)
 
     @pl.loop(0, 4)
     def _(n):
@@ -277,7 +300,7 @@
     for half in range(2):
         arrived(3 + half, r3.at[half])
         z[0:2048, :] = r3[half].astype(F32).reshape(2048, 128)
-        gather_pixels(z, 8, low, half * 256)
+        gather_pixels(z, 8, half, raw, low, swap)
         rows = slice(half * 256, (half + 1) * 256)
 
         @pl.loop(0, 4)
@@ -299,13 +322,13 @@
 
 
 def exchange(frames, probe):
-    wy, wx, perm, det = (jnp.asarray(t) for t in tables())
+    wy, wx, perm, swap, det = (jnp.asarray(t) for t in tables())
     hbm = pl.BlockSpec(memory_space=pl.ANY)
     dma = pltpu.SemaphoreType.DMA
     return pl.pallas_call(
         exchange_kernel,
-        out_shape=(jax.ShapeDtypeStruct((2, 512, 1024), BF16), jax.ShapeDtypeStruct((2, 64, 1024), F32)),
-        in_specs=[hbm] * 6,
+        out_shape=(jax.ShapeDtypeStruct((2, 512, 1024), BF16), jax.ShapeDtypeStruct((2, 8, 2, 8, 1024), F32)),
+        in_specs=[hbm] * 7,
         out_specs=(hbm, hbm),
         scratch_shapes=[
             pltpu.VMEM((512, 1024), BF16),
@@ -314,6 +337,7 @@
             pltpu.VMEM((512, 1024), BF16),
             pltpu.VMEM((2, 256, 512), BF16),
             pltpu.VMEM((512, 512), BF16),
+            pltpu.VMEM((256, 256), BF16),
             pltpu.VMEM((4, 32, 1024), F32),
             pltpu.VMEM((4, 512, 128), F32),
             pltpu.VMEM((4096, 128), F32),
@@ -326,60 +350,51 @@
             pltpu.VMEM((16, 32, 8, 128), BF16),
             pltpu.VMEM((4096, 128), BF16),
             pltpu.VMEM((2, 256, 8, 128), BF16),
+            pltpu.VMEM((256, 1024), BF16),
             pltpu.VMEM((512, 1024), BF16),
             pltpu.VMEM((2, 1024, 1024), BF16),
             pltpu.VMEM((2, 1024, 1024), BF16),
             pltpu.VMEM((2, 64, 1024), F32),
             pltpu.VMEM((2, 64, 1024), F32),
+            pltpu.VMEM((2, 8, 2, 8, 1024), F32),
             pltpu.VMEM((4, 512, 256), F32),
             pltpu.VMEM((4, 512, 256), F32),
             pltpu.VMEM((2, 512, 1024), BF16),
-            dma((6,)), dma, dma, dma((5,)), dma((5,)), dma((3,)),
+            dma((7,)), dma, dma, dma((5,)), dma((5,)), dma((3,)),
         ],
         compiler_params=pltpu.CompilerParams(collective_id=0, has_side_effects=True, vmem_limit_bytes=60 << 20),
-    )(frames, probe, wy, wx, perm, det)
+    )(frames, probe, wy, wx, perm, swap, det)
 
 
 def quotient_kernel(spec, gain, out_re, out_im):
-    row = lax.broadcasted_iota(jnp.int32, (8, 128), 0)
-
-    @pl.loop(0, 8)
-    def _(j):
-        gains = []
-        for c in range(2):
-            tiles = []
-            for t in range(4):
-                first = jnp.broadcast_to(gain[c, pl.ds(16 * t + j, 1), :], (8, 128))
-                second = jnp.broadcast_to(gain[c, pl.ds(16 * t + 8 + j, 1), :], (8, 128))
-                tiles.append(jnp.where(row < 4, first, second))
-            gains.append(jnp.concatenate(tiles, axis=0))
-        g_re, g_im = gains
-        for w in range(2):
-            v = 2 * j + w
-            rows = pl.ds(pl.multiple_of(v * 32, 32), 32)
-            s_re, s_im = spec[0, rows, :].astype(F32), spec[1, rows, :].astype(F32)
-            out_re[pl.ds(v, 32, stride=16), :] = s_re * g_re + s_im * g_im
-            out_im[pl.ds(v, 32, stride=16), :] = s_im * g_re - s_re * g_im
+    @pl.loop(0, 2)
+    def _(i):
+        for half in range(2):
+            g_re, g_im = gain[0, i, half], gain[1, i, half]
+            for w in range(4):
+                u = 4 * i + w
+                s_re, s_im = spec[0, half, u].astype(F32), spec[1, half, u].astype(F32)
+                out_re[u, half * 8 : half * 8 + 8, :] = s_re * g_re + s_im * g_im
+                out_im[u, half * 8 : half * 8 + 8, :] = s_im * g_re - s_re * g_im
 
 
 def quotient(spec, gain):
     return pl.pallas_call(
         quotient_kernel,
-        grid=(8,),
-        out_shape=(jax.ShapeDtypeStruct((512, 1024), F32),) * 2,
+        grid=(4,),
+        out_shape=(jax.ShapeDtypeStruct((32, 16, 1024), F32),) * 2,
         in_specs=[
-            pl.BlockSpec((2, 512, 128), lambda n: (0, 0, n)),
-            pl.BlockSpec((2, 64, 128), lambda n: (0, 0, n)),
+            pl.BlockSpec((2, 2, 8, 8, 1024), lambda n: (0, 0, n, 0, 0)),
+            pl.BlockSpec((2, 2, 2, 8, 1024), lambda n: (0, n, 0, 0, 0)),
         ],
-        out_specs=(pl.BlockSpec((512, 128), lambda n: (0, n)),) * 2,
+        out_specs=(pl.BlockSpec((8, 16, 1024), lambda n: (n, 0, 0)),) * 2,
         compiler_params=pltpu.CompilerParams(vmem_limit_bytes=60 << 20),
-    )(spec, gain)
+    )(spec.reshape(2, 2, 32, 8, 1024), gain)
 
 
 def shards(frames, probe_wave):
     spec, gain = exchange(frames.reshape(512, PIX), probe_wave)
-    real, imag = quotient(spec, gain)
-    return real.reshape(32, 16, PIX), imag.reshape(32, 16, PIX)
+    return quotient(spec, gain)
 
 
 def solution(mesh):

time: 100 us -> 97.7 us (0.977)
  Pallas kernels: 99.5 us -> 96.9 us
    pallas_call x1, Pallas kernels: 7.02 us -> 4.54 us  [quotient(): pl.pallas_call(quotient_kernel, grid=(4,), out_shape=(jax.ShapeDtypeStruc...]
where the time goes in v3:
time: 97.7 us; the launch traced here: 97.5 us
  Pallas kernels  96.9 us (99%)
    pallas_call x1, Pallas kernels, exchange(): pl.pallas_call(exchange_kernel, out_shape=(jax.ShapeDtypeStruct((2, 512,...  92.3 us
    pallas_call x1, Pallas kernels, quotient(): pl.pallas_call(quotient_kernel, grid=(4,), out_shape=(jax.ShapeDtypeStruc...  4.54 us

profile of v3, /device:TPU:1, one launch (start us, length us, event | category | flops | bytes accessed | tf_op | source)
XLA Modules:
  0.0 97.5 jit_solution(9673521766403217393)
XLA Ops:
  0.6 92.3 %shard_map.86 = (bf16[2,512,1024]{2,1,0:T(8,128)(2,1)}, f32[2,8,2,8,1024]{4,3,2,1,0:T(8,128)}) custom-call(bf16[512,1024]{1,0:T(8,128)(2,1)} %bitcast.3, f32[2,8,128]{2,1,0:T(8,128)} %probe.1, bf16[512,1024]{1,0:T(8,128)(2,1)} %constant.10.clone.wy_h, bf16[2,256,512]{2,1,0:T(8,128)(2,1)} %constant.11.clone.wx_h, bf16[512,512]{1,0:T(8,128)(2,1)} %constant.12.clone.perm_h, ...), custom_call_target="tpu_custom_call" | custom-call | tf_op jit(solution)/shard_map/pallas_call | solution.py:328
  93.0 4.5 %shard_map.87 = (f32[32,16,1024]{2,1,0:T(8,128)}, f32[32,16,1024]{2,1,0:T(8,128)}) custom-call(bf16[2,2,32,8,1024]{4,3,2,1,0:T(8,128)(2,1)} %bitcast.2, f32[2,8,2,8,1024]{4,3,2,1,0:T(8,128)} %get-tuple-element.5.gain), custom_call_target="tpu_custom_call" | custom-call | tf_op jit(solution)/shard_map/pallas_call | solution.py:382

commit v4 on v3

--- a/solution.py
+++ b/solution.py
@@ -178,22 +178,26 @@
             store(4 * t + q, res[:, q * 128 : (q + 1) * 128])
 
 
-def gather_pixels(z, count, half, raw, low, swap):
-    @pl.loop(0, 8)
-    def _(v):
+def gather_pixels(z, count, half, raw, low, swap, unroll):
+    def gather(v):
         first = v + 8 * half if count == 16 else v
         halves = [z[pl.ds(dh * 128 * count + first, 128, stride=count), :].T for dh in range(2)]
         turned = jnp.concatenate(halves, axis=1).astype(BF16)
         rows = jnp.concatenate([turned[s * 32 : (s + 1) * 32, :] for s in range(4)], axis=1)
-        raw[pl.ds(pl.multiple_of(v * 32, 32), 32), :] = rows
-
+        raw[pl.ds(v * 32 if unroll else pl.multiple_of(v * 32, 32), 32), :] = rows
+
+    if unroll:
+        for v in range(8):
+            gather(v)
+    else:
+        pl.loop(0, 8)(gather)
     low[half * 256 : (half + 1) * 256, :] = dot(swap[...], raw[...]).astype(BF16)
 
 
 def exchange_kernel(
-    frames, probe, wy_h, wx_h, perm_h, swap_h, det_h, spec_out, gain_out,
-    x, pv, prb, wy, wx, perm, swap, det, xs, z, m1, r, rp, cst, f, m2, m3, r2, r3, raw, low, ddr, ddi, pf, chi, gain, sre, sim, spec,
-    load_sem, prb_send, prb_recv, send, recv, out_sem,
+    frames, probe, wy_h, wx_h, perm_h, swap_h, det_h, spec, gain,
+    x, pv, prb, wy, wx, perm, swap, det, xs, z, m1, r, rp, cst, f, m2, m3, r2, r3, raw, low, ddr, ddi, pf, chi, sre, sim,
+    load_sem, prb_send, prb_recv, send, recv,
 ):
     g, m = lax.axis_index("grp"), lax.axis_index("mem")
     me = g * 16 + m
@@ -282,13 +286,11 @@
     pltpu.make_async_copy(prb, prb, prb_recv).wait()
     probe_products(g, m, prb, pf)
     wiener_gain(pf, ddr, ddi, chi, gain)
-    gain_copy = pltpu.make_async_copy(gain, gain_out, out_sem.at[0])
-    gain_copy.start()
 
     arrived(2, r2)
     z[...] = r2[...].astype(F32)
     for half in range(2):
-        gather_pixels(z, 16, half, raw, low, swap)
+        gather_pixels(z, 16, half, raw, low, swap, False)
 
     @pl.loop(0, 4)
     def _(n):
@@ -296,40 +298,34 @@
         sre[n] = dot(low[...], ddr[0, :, lanes])
         sim[n] = dot(low[...], ddi[0, :, lanes])
 
-    copies = []
     for half in range(2):
         arrived(3 + half, r3.at[half])
         z[0:2048, :] = r3[half].astype(F32).reshape(2048, 128)
-        gather_pixels(z, 8, half, raw, low, swap)
+        gather_pixels(z, 8, half, raw, low, swap, half == 1)
         rows = slice(half * 256, (half + 1) * 256)
 
-        @pl.loop(0, 4)
-        def _(n):
-            lanes = pl.ds(pl.multiple_of(n * 256, 256), 256)
+        for n in range(4):
+            lanes = slice(n * 256, (n + 1) * 256)
             spec[0, rows, lanes] = (sre[n, rows, :] + dot(low[rows, :], ddr[1, :, lanes])).astype(BF16)
             spec[1, rows, lanes] = (sim[n, rows, :] + dot(low[rows, :], ddi[1, :, lanes])).astype(BF16)
 
-        copies.append(pltpu.make_async_copy(spec.at[:, rows], spec_out.at[:, rows], out_sem.at[1 + half]))
-        copies[-1].start()
 
     pltpu.make_async_copy(prb.at[pl.ds(0, 15)], prb.at[pl.ds(0, 15)], prb_send).wait()
     for n, ref in enumerate((r.at[0], r.at[1], None, r3.at[0], r3.at[1])):
         ref = r2.at[pl.ds(0, 255 * 16)] if ref is None else ref.at[pl.ds(0, 255)]
         pltpu.make_async_copy(ref, ref, send.at[n]).wait()
-    gain_copy.wait()
-    for copy in copies:
-        copy.wait()
 
 
 def exchange(frames, probe):
     wy, wx, perm, swap, det = (jnp.asarray(t) for t in tables())
     hbm = pl.BlockSpec(memory_space=pl.ANY)
+    vmem = pl.BlockSpec(memory_space=pltpu.VMEM)
     dma = pltpu.SemaphoreType.DMA
     return pl.pallas_call(
         exchange_kernel,
-        out_shape=(jax.ShapeDtypeStruct((2, 512, 1024), BF16), jax.ShapeDtypeStruct((2, 8, 2, 8, 1024), F32)),
+        out_shape=(pltpu.VMEM((2, 512, 1024), BF16), pltpu.VMEM((2, 8, 2, 8, 1024), F32)),
         in_specs=[hbm] * 7,
-        out_specs=(hbm, hbm),
+        out_specs=(vmem, vmem),
         scratch_shapes=[
             pltpu.VMEM((512, 1024), BF16),
             pltpu.VMEM((2, 8, 128), F32),
@@ -356,40 +352,36 @@
             pltpu.VMEM((2, 1024, 1024), BF16),
             pltpu.VMEM((2, 64, 1024), F32),
             pltpu.VMEM((2, 64, 1024), F32),
-            pltpu.VMEM((2, 8, 2, 8, 1024), F32),
             pltpu.VMEM((4, 512, 256), F32),
             pltpu.VMEM((4, 512, 256), F32),
-            pltpu.VMEM((2, 512, 1024), BF16),
-            dma((7,)), dma, dma, dma((5,)), dma((5,)), dma((3,)),
+            dma((7,)), dma, dma, dma((5,)), dma((5,)),
         ],
-        compiler_params=pltpu.CompilerParams(collective_id=0, has_side_effects=True, vmem_limit_bytes=60 << 20),
+        compiler_params=pltpu.CompilerParams(collective_id=0, has_side_effects=True, vmem_limit_bytes=52 << 20),
     )(frames, probe, wy, wx, perm, swap, det)
 
 
 def quotient_kernel(spec, gain, out_re, out_im):
-    @pl.loop(0, 2)
-    def _(i):
-        for half in range(2):
-            g_re, g_im = gain[0, i, half], gain[1, i, half]
-            for w in range(4):
-                u = 4 * i + w
-                s_re, s_im = spec[0, half, u].astype(F32), spec[1, half, u].astype(F32)
-                out_re[u, half * 8 : half * 8 + 8, :] = s_re * g_re + s_im * g_im
-                out_im[u, half * 8 : half * 8 + 8, :] = s_im * g_re - s_re * g_im
+    n = pl.program_id(0)
+    for half in range(2):
+        g_re, g_im = gain[0, n, half], gain[1, n, half]
+        rows = pl.ds(pl.multiple_of(half * 256 + n * 32, 32), 32)
+        s_re, s_im = spec[0, rows, :].astype(F32), spec[1, rows, :].astype(F32)
+        for u in range(4):
+            a, b = s_re[u * 8 : u * 8 + 8, :], s_im[u * 8 : u * 8 + 8, :]
+            out_re[u, half * 8 : half * 8 + 8, :] = a * g_re + b * g_im
+            out_im[u, half * 8 : half * 8 + 8, :] = b * g_re - a * g_im
 
 
 def quotient(spec, gain):
+    vmem = pl.BlockSpec(memory_space=pltpu.VMEM)
     return pl.pallas_call(
         quotient_kernel,
-        grid=(4,),
+        grid=(8,),
         out_shape=(jax.ShapeDtypeStruct((32, 16, 1024), F32),) * 2,
-        in_specs=[
-            pl.BlockSpec((2, 2, 8, 8, 1024), lambda n: (0, 0, n, 0, 0)),
-            pl.BlockSpec((2, 2, 2, 8, 1024), lambda n: (0, n, 0, 0, 0)),
-        ],
-        out_specs=(pl.BlockSpec((8, 16, 1024), lambda n: (n, 0, 0)),) * 2,
-        compiler_params=pltpu.CompilerParams(vmem_limit_bytes=60 << 20),
-    )(spec.reshape(2, 2, 32, 8, 1024), gain)
+        in_specs=[vmem, vmem],
+        out_specs=(pl.BlockSpec((4, 16, 1024), lambda n: (n, 0, 0)),) * 2,
+        compiler_params=pltpu.CompilerParams(vmem_limit_bytes=16 << 20),
+    )(spec, gain)
 
 
 def shards(frames, probe_wave):

time: 97.7 us -> 94.3 us (0.965)
  Pallas kernels: 96.9 us -> 93.6 us
    pallas_call x2, Pallas kernels: 96.9 us -> 93.6 us  [the longest x1 89.9 us: exchange(): pl.pallas_call(exchange_kernel, out_shape=(pltpu.VMEM((2, 512, 1024), BF1...]
where the time goes in v4:
time: 94.3 us; the launch traced here: 94.2 us
  Pallas kernels  93.6 us (99%)
    pallas_call x1, Pallas kernels, exchange(): pl.pallas_call(exchange_kernel, out_shape=(pltpu.VMEM((2, 512, 1024), BF1...  89.9 us
    pallas_call x1, Pallas kernels, quotient(): pl.pallas_call(quotient_kernel, grid=(8,), out_shape=(jax.ShapeDtypeStruc...  3.62 us

profile of v4, /device:TPU:1, one launch (start us, length us, event | category | flops | bytes accessed | tf_op | source)
XLA Modules:
  0.0 94.2 jit_solution(13504997943742963511)
XLA Ops:
  0.6 89.9 %shard_map.86 = (bf16[2,512,1024]{2,1,0:T(8,128)(2,1)S(1)}, f32[2,8,2,8,1024]{4,3,2,1,0:T(8,128)S(1)}) custom-call(bf16[512,1024]{1,0:T(8,128)(2,1)} %bitcast.1, f32[2,8,128]{2,1,0:T(8,128)} %probe.1, bf16[512,1024]{1,0:T(8,128)(2,1)} %constant.10.clone.wy_h, bf16[2,256,512]{2,1,0:T(8,128)(2,1)} %constant.11.clone.wx_h, ...), custom_call_target="tpu_custom_call" | custom-call | tf_op jit(solution)/shard_map/pallas_call | solution.py:324
  90.6 3.6 %shard_map.87 = (f32[32,16,1024]{2,1,0:T(8,128)}, f32[32,16,1024]{2,1,0:T(8,128)}) custom-call(bf16[2,512,1024]{2,1,0:T(8,128)(2,1)S(1)} %get-tuple-element.4.spec, f32[2,8,2,8,1024]{4,3,2,1,0:T(8,128)S(1)} %get-tuple-element.5.gain), custom_call_target="tpu_custom_call" | custom-call | tf_op jit(solution)/shard_map/pallas_call | solution.py:377

commit v5 on v4

--- a/solution.py
+++ b/solution.py
@@ -242,11 +242,12 @@
 
     loads[0].wait()
     loads[1].wait()
+    arrange_frames(0, x, xs, z, m1)
+    pl.semaphore_wait(barrier, 255)
+
     for h in range(2):
-        arrange_frames(h, x, xs, z, m1)
-    pl.semaphore_wait(barrier, 255)
-
-    for h in range(2):
+        if h == 1:
+            arrange_frames(1, x, xs, z, m1)
         pltpu.make_async_copy(m1.at[h, me], r.at[h, me], recv.at[h]).start()
         to_all(lambda a, b: push(h, m1.at[h, a * 16 + b], r.at[h, me], a, b))
         if h == 0:

time: 94.3 us -> 94.3 us (level)
  no operation moved by 1% of the time
where the time goes in v5:
time: 94.3 us; the launch traced here: 94.2 us
  Pallas kernels  93.6 us (99%)
    pallas_call x1, Pallas kernels, exchange(): pl.pallas_call(exchange_kernel, out_shape=(pltpu.VMEM((2, 512, 1024), BF1...  89.9 us
    pallas_call x1, Pallas kernels, quotient(): pl.pallas_call(quotient_kernel, grid=(8,), out_shape=(jax.ShapeDtypeStruc...  3.62 us

profile of v5, /device:TPU:1, one launch (start us, length us, event | category | flops | bytes accessed | tf_op | source)
XLA Modules:
  0.0 94.2 jit_solution(9710921412472951810)
XLA Ops:
  0.6 89.9 %shard_map.86 = (bf16[2,512,1024]{2,1,0:T(8,128)(2,1)S(1)}, f32[2,8,2,8,1024]{4,3,2,1,0:T(8,128)S(1)}) custom-call(bf16[512,1024]{1,0:T(8,128)(2,1)} %bitcast.1, f32[2,8,128]{2,1,0:T(8,128)} %probe.1, bf16[512,1024]{1,0:T(8,128)(2,1)} %constant.10.clone.wy_h, bf16[2,256,512]{2,1,0:T(8,128)(2,1)} %constant.11.clone.wx_h, ...), custom_call_target="tpu_custom_call" | custom-call | tf_op jit(solution)/shard_map/pallas_call | solution.py:325
  90.6 3.6 %shard_map.87 = (f32[32,16,1024]{2,1,0:T(8,128)}, f32[32,16,1024]{2,1,0:T(8,128)}) custom-call(bf16[2,512,1024]{2,1,0:T(8,128)(2,1)S(1)} %get-tuple-element.4.spec, f32[2,8,2,8,1024]{4,3,2,1,0:T(8,128)S(1)} %get-tuple-element.5.gain), custom_call_target="tpu_custom_call" | custom-call | tf_op jit(solution)/shard_map/pallas_call | solution.py:378

commit v6 on v5

--- a/solution.py
+++ b/solution.py
@@ -150,15 +150,26 @@
                 gain[c, i, half] = tile
 
 
+def unrolled(count):
+    def run(act):
+        for i in range(count):
+            act(i)
+
+    return run
+
+
 def scan_transform(h, r, rp, cst, f, store, wy, wx, perm):
-    @pl.loop(0, 4)
+    def loop(count):
+        return unrolled(count) if h == 0 else pl.loop(0, count)
+
+    @loop(4)
     def _(j):
         parts = [r[h, pl.ds((4 * j + t) * 16, 16)].astype(F32).reshape(128, 128) for t in range(4)]
         moved = dot(jnp.concatenate(parts, axis=1).astype(BF16), perm[...]).astype(BF16)
         for s in range(4):
             rp[s, j] = moved[:, s * 128 : (s + 1) * 128]
 
-    @pl.loop(0, 2)
+    @loop(2)
     def _(k2):
         lhs = jnp.concatenate(
             [jnp.concatenate([rp[2 * k2 + x2, j] for j in range(4)], axis=1) for x2 in range(2)], axis=0
@@ -170,7 +181,7 @@
             for t in range(4):
                 f[t, 2 * c + k2] = res[:, t * 128 : (t + 1) * 128]
 
-    @pl.loop(0, 4)
+    @loop(4)
     def _(t):
         lhs = jnp.concatenate([f[t, s] for s in range(4)], axis=1)
         res = dot(lhs, perm[...])

time: 94.3 us -> 94.3 us (level)
  no operation moved by 1% of the time
where the time goes in v6:
time: 94.3 us; the launch traced here: 94.2 us
  Pallas kernels  93.6 us (99%)
    pallas_call x1, Pallas kernels, exchange(): pl.pallas_call(exchange_kernel, out_shape=(pltpu.VMEM((2, 512, 1024), BF1...  89.9 us
    pallas_call x1, Pallas kernels, quotient(): pl.pallas_call(quotient_kernel, grid=(8,), out_shape=(jax.ShapeDtypeStruc...  3.62 us

profile of v6, /device:TPU:1, one launch (start us, length us, event | category | flops | bytes accessed | tf_op | source)
XLA Modules:
  0.0 94.2 jit_solution(12327417792306256251)
XLA Ops:
  0.6 89.9 %shard_map.86 = (bf16[2,512,1024]{2,1,0:T(8,128)(2,1)S(1)}, f32[2,8,2,8,1024]{4,3,2,1,0:T(8,128)S(1)}) custom-call(bf16[512,1024]{1,0:T(8,128)(2,1)} %bitcast.1, f32[2,8,128]{2,1,0:T(8,128)} %probe.1, bf16[512,1024]{1,0:T(8,128)(2,1)} %constant.10.clone.wy_h, bf16[2,256,512]{2,1,0:T(8,128)(2,1)} %constant.11.clone.wx_h, ...), custom_call_target="tpu_custom_call" | custom-call | tf_op jit(solution)/shard_map/pallas_call | solution.py:336
  90.6 3.6 %shard_map.87 = (f32[32,16,1024]{2,1,0:T(8,128)}, f32[32,16,1024]{2,1,0:T(8,128)}) custom-call(bf16[2,512,1024]{2,1,0:T(8,128)(2,1)S(1)} %get-tuple-element.4.spec, f32[2,8,2,8,1024]{4,3,2,1,0:T(8,128)S(1)} %get-tuple-element.5.gain), custom_call_target="tpu_custom_call" | custom-call | tf_op jit(solution)/shard_map/pallas_call | solution.py:389
